TPU v7x, 1024 devices: a whole 4x8x16 slice. The times are simulated.
1024 devices in a mesh: dp: 128 (over y_hi, z, core), section: 8 (over y_lo, x).
Axes of the slice: x: 4, y: 8 (y_hi: 4, y_lo: 2; y = y_hi * 2 + y_lo), z: 16, core: 2. Of those that a mesh axis runs over, the one named last changes fastest.
Arguments:
- layer_inputs: bfloat16 [8, 2, 256, 32, 4096], P('section', None, 'dp'), may hold values from -6 to 6
- saved_queries: bfloat16 [8, 2, 256, 32, 128], P('section', None, 'dp'), may hold values from -16 to 16
- saved_keys: bfloat16 [8, 2, 256, 32, 128], P('section', None, 'dp'), may hold values from -16 to 16
- held_weights: bfloat16 [8, 2, 2, 4096, 128], P('section'), may hold values from -0.15625 to 0.15625
- cotangent: bfloat16 [2, 256, 32, 4096], P(None, 'dp'), may hold values from -6 to 6
- valid_lengths: int32 [2, 256], P(None, 'dp'), may hold values from 2 to 32, as said below
Outputs:
- input_grads: bfloat16 [8, 2, 256, 32, 4096], P('section', None, 'dp')
- weight_grads: float32 [8, 2, 4096, 128], P('section', None, 'dp')
Inputs may be any that keep to these rules, and one draw needn't show every extreme that they name: `valid_lengths`: some sequence has 32 valid tokens.
All inputs are finite; a program needn't handle non-finite values.
Results may differ from a plain program's by a relative error of at most 0.014.
Values may be sent and summed in bfloat16 or wider, within the bound.
A program may use at most 64 MiB of HBM per device.

v0:
```python
import math

import jax
import jax.numpy as jnp
from jax import lax
from jax.sharding import Mesh
from jax.sharding import PartitionSpec as P

SECTION = ("section_0", "section_1")
DP = ("dp_0", "dp_1", "dp_2")


def passed_along(block, axis, distance):
    devices = range(lax.axis_size(axis))
    route = [(i - distance, i) for i in devices if i - distance in devices]
    return lax.ppermute(block, axis, route)


def sum_in_order(blocks, axes, sequence):
    lengths = [lax.axis_size(a) for a in axes]
    blocks = blocks.reshape(*lengths, *blocks.shape[1:])
    blocks = blocks.transpose(*sequence, *range(len(axes), blocks.ndim))
    blocks = blocks.reshape(-1, *blocks.shape[len(axes) :])
    for k in sequence:
        blocks = lax.psum_scatter(blocks, axes[k], scatter_dimension=0, tiled=True)
    return blocks[0]


def in_blocks(x, dim, length):
    before, after = (x.shape[:dim], x.shape[dim + 1 :])
    return jnp.moveaxis(x.reshape(*before, length, -1, *after), dim, 0)


def sum_by_axis_2(x, axes, sequence, dim):
    length = lax.axis_size(axes)
    return sum_in_order(in_blocks(x, dim, length), axes, sequence)


def laid_out(blocks, dim):
    blocks = jnp.moveaxis(blocks, 0, dim)
    lengths = blocks.shape
    return blocks.reshape(*lengths[:dim], lengths[dim] * lengths[dim + 1], *lengths[dim + 2 :])


def stacked_from(x, axes, sequence):
    blocks = x
    for k in sequence:
        blocks = lax.all_gather(blocks, axes[k])
    done = sequence[::-1]
    back = [done.index(k) for k in range(len(axes))]
    blocks = blocks.transpose(*back, *range(len(axes), blocks.ndim))
    return blocks.reshape(-1, *x.shape)


def gathered_by_axis(x, axes, sequence, dim):
    return laid_out(stacked_from(x, axes, sequence), dim)


def attention_weights(queries, key_vectors, valid_lengths):
    length = queries.shape[-2]
    scores = jnp.einsum(
        "nmth,nmsh->nmts", queries, key_vectors, preferred_element_type=jnp.float32
    ) / math.sqrt(queries.shape[-1])
    row_pos = lax.broadcasted_iota(jnp.int32, (length, length), 0)
    col_pos = lax.broadcasted_iota(jnp.int32, (length, length), 1)
    allowed = (col_pos <= row_pos)[None, None] & (
        col_pos[None, None] < valid_lengths[:, :, None, None]
    )
    scores = jnp.where(allowed, scores, -jnp.inf)
    row_max = jnp.max(scores, axis=-1, keepdims=True)
    raised = jnp.where(allowed, jnp.exp(scores - row_max), 0.0)
    return (raised / jnp.sum(raised, axis=-1, keepdims=True)).astype(jnp.bfloat16)


def shards(layer_inputs, saved_queries, saved_keys, held_weights, cotangent, valid_lengths):
    sections = lax.axis_size(SECTION)
    position = lax.axis_index(SECTION)
    inputs = layer_inputs[0]
    value_w = held_weights[0, :, 0]
    output_w = held_weights[0, :, 1]
    attend = attention_weights(saved_queries[0], saved_keys[0], valid_lengths)
    micro_count = inputs.shape[1]
    length = inputs.shape[2]
    model_width = inputs.shape[3]
    head_size = value_w.shape[2]
    values = jnp.einsum(
        "nmld,ndh->nmlh", inputs, value_w, preferred_element_type=jnp.float32
    ).astype(jnp.bfloat16)
    mixtures = jnp.einsum(
        "nmts,nmsh->nmth", attend, values, preferred_element_type=jnp.float32
    ).astype(jnp.bfloat16)
    is_end = [position == sections - 1, position == 0]
    starts = [sections - 1 - position, position]

    def make_compute(direction):

        def compute(operands):
            grads, uppers, vgrads, incoming, index = operands
            fresh = lax.dynamic_index_in_dim(cotangent[direction], index, 0, keepdims=False)
            upstream = jnp.where(is_end[direction], fresh, incoming)
            weights_now = lax.dynamic_index_in_dim(attend[direction], index, 0, keepdims=False)
            out_grad = jnp.dot(
                upstream, output_w[direction], preferred_element_type=jnp.float32
            ).astype(jnp.bfloat16)
            val_grad = jnp.einsum(
                "ts,th->sh", weights_now, out_grad, preferred_element_type=jnp.float32
            ).astype(jnp.bfloat16)
            branch = jnp.einsum(
                "lh,dh->ld", val_grad, value_w[direction], preferred_element_type=jnp.float32
            )
            grad_input = (upstream.astype(jnp.float32) + branch).astype(jnp.bfloat16)
            grads = lax.dynamic_update_index_in_dim(grads, grad_input, index, 0)
            uppers = lax.dynamic_update_index_in_dim(uppers, upstream, index, 0)
            vgrads = lax.dynamic_update_index_in_dim(vgrads, val_grad, index, 0)
            return (grad_input, (grads, uppers, vgrads))

        return compute

    def skip(operands):
        grads, uppers, vgrads, incoming, index = operands
        return (jnp.zeros_like(incoming), (grads, uppers, vgrads))

    def advance(moment, received, buffers):
        outgoing = []
        updated = []
        for direction in range(2):
            micro_id = moment - starts[direction]
            active = (micro_id >= 0) & (micro_id < micro_count)
            clipped = jnp.clip(micro_id, 0, micro_count - 1)
            grads, uppers, vgrads = buffers[direction]
            sent_now, fresh_buffers = lax.cond(
                active,
                make_compute(direction),
                skip,
                (grads, uppers, vgrads, received[direction], clipped),
            )
            outgoing.append(sent_now)
            updated.append(fresh_buffers)
        return (jnp.stack(outgoing), tuple(updated))

    big_zero = jnp.zeros((micro_count, length, model_width), jnp.bfloat16)
    small_zero = jnp.zeros((micro_count, length, head_size), jnp.bfloat16)
    buffers = ((big_zero, big_zero, small_zero), (big_zero, big_zero, small_zero))
    sent, buffers = advance(
        jnp.int32(0), jnp.zeros((2, length, model_width), jnp.bfloat16), buffers
    )

    def loop_body(moment, carried):
        outgoing, held = carried
        from_next = passed_along(outgoing[0], SECTION, -1)
        from_prev = passed_along(outgoing[1], SECTION, 1)
        return advance(moment, jnp.stack([from_next, from_prev]), held)

    sent, buffers = lax.fori_loop(1, sections + micro_count - 1, loop_body, (sent, buffers))
    grads_in = jnp.stack([buffers[0][0], buffers[1][0]])
    upstreams = jnp.stack([buffers[0][1], buffers[1][1]])
    val_grads = jnp.stack([buffers[0][2], buffers[1][2]])
    flat_in = inputs.reshape(2, micro_count * length, model_width)
    flat_up = upstreams.reshape(2, micro_count * length, model_width)
    flat_mix = mixtures.reshape(2, micro_count * length, head_size)
    flat_vg = val_grads.reshape(2, micro_count * length, head_size)
    grad_value = jnp.einsum("ntd,nth->dnh", flat_in, flat_vg, preferred_element_type=jnp.float32)
    grad_output = jnp.einsum("ntd,nth->dnh", flat_up, flat_mix, preferred_element_type=jnp.float32)
    summed = sum_by_axis_2(
        jnp.stack([grad_value, grad_output], axis=2).reshape(
            model_width // lax.axis_size(DP) * lax.axis_size(DP), 4 * head_size
        ),
        DP,
        (2, 1, 0),
        0,
    )
    summed = summed.reshape(-1, 2, 2, head_size)
    own_part = summed[:, 0]
    mirror_part = summed[:, 1]
    gathered = gathered_by_axis(mirror_part[None].astype(jnp.bfloat16), SECTION, (0, 1), 0).astype(
        jnp.float32
    )
    mirror_part = lax.dynamic_index_in_dim(gathered, sections - 1 - position, 0, keepdims=False)
    combined = own_part + mirror_part
    weight_grads = jnp.transpose(combined, (1, 0, 2))[None]
    return (grads_in[None], weight_grads)


def solution(mesh):
    finer = Mesh(
        mesh.devices.reshape(4, 16, 2, 2, 4), ("dp_0", "dp_1", "dp_2", "section_0", "section_1")
    )
    in_specs = (
        P(SECTION, None, DP, None, None),
        P(SECTION, None, DP, None, None),
        P(SECTION, None, DP, None, None),
        P(SECTION, None, None, None, None),
        P(None, DP, None, None),
        P(None, DP),
    )
    out_specs = (P(SECTION, None, DP, None, None), P(SECTION, None, DP, None))
    return jax.shard_map(
        shards, mesh=finer, in_specs=in_specs, out_specs=out_specs, check_vma=False
    )
```

profile of v0, /device:TPU:1, one launch (start us, length us, event | category | flops | bytes accessed | tf_op | source)
XLA Modules:
  0.0 431.2 jit_solution(14879819501623653335)
XLA Ops:
  8.4 3.8 slice_bitcast_fusion.3
  12.2 2.2 convolution_convert_fusion.8
  14.4 2.3 conditional.4
  16.8 9.5 %conditional.5 = (bf16[2,32,4096]{2,1,0:T(8,128)(2,1)}, bf16[2,32,4096]{2,1,0:T(8,128)(2,1)}, bf16[2,32,128]{2,1,0:T(8,128)(2,1)}, bf16[1,32,4096]{2,1,0:T(8,128)(2,1)}) conditional(s32[]{:T(128)} %convert_element_type.107, () %tuple.64, (pred[]{:T(512)}, bf16[2,2,32,4096]{3,2,1,0:T(8,128)(2,1)}, s32[]{:T(128)}, bf16[2,2,32,32]{2,3,1,0:T(8,128)(2,1)S(1)}, ...), branch_computations={%region_4.5_spmd, %region_5.6_spmd} | conditional | flops 68165632 | bytes 7941252 | solution.py:131
  16.9 1.9 slice.57
  19.4 2.3 bitcast_dynamic-update-slice_fusion.3
  22.5 2.2 constant_dynamic-update-slice_fusion.1
  26.3 1.8 pad_maximum_fusion.2
  28.1 169.4 %while.25 = (s32[]{:T(128)}, bf16[2,32,4096]{2,1,0:T(8,128)(2,1)}, bf16[2,32,4096]{2,1,0:T(8,128)(2,1)}, bf16[2,32,4096]{2,1,0:T(8,128)(2,1)}, bf16[2,32,128]{2,...) while((s32[]{:T(128)}, bf16[2,32,4096]{2,1,0:T(8,128)(2,1)}, ...), condition=%wide.region_11.12_spmd, body=%wide.region_6.11_spmd.sunk | while | flops 136069120 | bytes 15814325 | solution.py:154
  28.1 1.9 slice_bitcast_fusion.6
  30.0 1.3 collective-permute-start.1
  31.3 4.7 %collective-permute-start = (bf16[32,4096]{1,0:T(8,128)(2,1)}, bf16[32,4096]{1,0:T(8,128)(2,1)}, u32[]{:S(2)}, u32[]{:S(2)}) collective-permute-start(bf16[32,4096]{1,0:T(8,128)(2,1)} %get-tuple-element.707), channel_id=1, source_target_pairs={{0,1},{1,2},{2,3},{3,4},{4,5},{5,6},{6,7},{8,9},{9,10},{10,11},{11... | collective-permute-start | bytes 786440 | tf_op jit(solution)/shard_map/while/body/eval_jaxpr/ppermute | solution.py:16
  36.0 1.3 collective-permute-done.1
  38.9 5.3 %conditional.8 = (bf16[2,32,4096]{2,1,0:T(8,128)(2,1)}, bf16[2,32,4096]{2,1,0:T(8,128)(2,1)}, bf16[2,32,128]{2,1,0:T(8,128)(2,1)}, bf16[1,32,4096]{2,1,0:T(8,128)(2,1)}) conditional(s32[]{:T(128)} %convert_element_type.164, (bf16[2,32,4096]{2,1,0:T(8,128)(2,1)}, bf16[2,32,4096]{2,1,0:T(8,128)(2,1)}, bf16[2,32,128]{2,1,0:T(8,128)(2,1)}) %tuple.106, ...), branch_computations={%region_9.9_spmd, %region_10.10_spmd} | conditional | flops 67903488 | bytes 5285440 | solution.py:131
  40.7 2.2 bitcast_dynamic-update-slice_fusion.7
  44.2 1.9 pad_maximum_fusion.4
  46.1 1.9 slice_bitcast_fusion.6
  48.0 1.3 collective-permute-start.1
  49.3 6.1 %collective-permute-start = (bf16[32,4096]{1,0:T(8,128)(2,1)}, bf16[32,4096]{1,0:T(8,128)(2,1)}, u32[]{:S(2)}, u32[]{:S(2)}) collective-permute-start(bf16[32,4096]{1,0:T(8,128)(2,1)} %get-tuple-element.707), channel_id=1, source_target_pairs={{0,1},{1,2},{2,3},{3,4},{4,5},{5,6},{6,7},{8,9},{9,10},{10,11},{11... | collective-permute-start | bytes 786440 | tf_op jit(solution)/shard_map/while/body/eval_jaxpr/ppermute | solution.py:16
  55.3 1.3 collective-permute-done.1
  59.0 1.9 pad_maximum_fusion.4
  60.9 1.9 slice_bitcast_fusion.6
  62.7 1.3 collective-permute-start.1
  64.0 10.7 %collective-permute-start = (bf16[32,4096]{1,0:T(8,128)(2,1)}, bf16[32,4096]{1,0:T(8,128)(2,1)}, u32[]{:S(2)}, u32[]{:S(2)}) collective-permute-start(bf16[32,4096]{1,0:T(8,128)(2,1)} %get-tuple-element.707), channel_id=1, source_target_pairs={{0,1},{1,2},{2,3},{3,4},{4,5},{5,6},{6,7},{8,9},{9,10},{10,11},{11... | collective-permute-start | bytes 786440 | tf_op jit(solution)/shard_map/while/body/eval_jaxpr/ppermute | solution.py:16
  74.7 1.3 collective-permute-done.1
  78.4 1.9 pad_maximum_fusion.4
  80.3 1.9 slice_bitcast_fusion.6
  83.4 5.1 %collective-permute-start = (bf16[32,4096]{1,0:T(8,128)(2,1)}, bf16[32,4096]{1,0:T(8,128)(2,1)}, u32[]{:S(2)}, u32[]{:S(2)}) collective-permute-start(bf16[32,4096]{1,0:T(8,128)(2,1)} %get-tuple-element.707), channel_id=1, source_target_pairs={{0,1},{1,2},{2,3},{3,4},{4,5},{5,6},{6,7},{8,9},{9,10},{10,11},{11... | collective-permute-start | bytes 786440 | tf_op jit(solution)/shard_map/while/body/eval_jaxpr/ppermute | solution.py:16
  88.6 1.3 collective-permute-done.1
  92.2 1.9 pad_maximum_fusion.4
  94.1 1.9 slice_bitcast_fusion.6
  97.2 11.1 %collective-permute-start = (bf16[32,4096]{1,0:T(8,128)(2,1)}, bf16[32,4096]{1,0:T(8,128)(2,1)}, u32[]{:S(2)}, u32[]{:S(2)}) collective-permute-start(bf16[32,4096]{1,0:T(8,128)(2,1)} %get-tuple-element.707), channel_id=1, source_target_pairs={{0,1},{1,2},{2,3},{3,4},{4,5},{5,6},{6,7},{8,9},{9,10},{10,11},{11... | collective-permute-start | bytes 786440 | tf_op jit(solution)/shard_map/while/body/eval_jaxpr/ppermute | solution.py:16
  108.4 2.8 collective-permute-done.1
  113.7 1.9 pad_maximum_fusion.4
  115.6 1.9 slice_bitcast_fusion.6
  118.7 5.3 %collective-permute-start = (bf16[32,4096]{1,0:T(8,128)(2,1)}, bf16[32,4096]{1,0:T(8,128)(2,1)}, u32[]{:S(2)}, u32[]{:S(2)}) collective-permute-start(bf16[32,4096]{1,0:T(8,128)(2,1)} %get-tuple-element.707), channel_id=1, source_target_pairs={{0,1},{1,2},{2,3},{3,4},{4,5},{5,6},{6,7},{8,9},{9,10},{10,11},{11... | collective-permute-start | bytes 786440 | tf_op jit(solution)/shard_map/while/body/eval_jaxpr/ppermute | solution.py:16
  124.1 1.3 collective-permute-done.1
  127.7 1.9 pad_maximum_fusion.4
  129.6 1.9 slice_bitcast_fusion.6
  132.8 25.5 %collective-permute-start = (bf16[32,4096]{1,0:T(8,128)(2,1)}, bf16[32,4096]{1,0:T(8,128)(2,1)}, u32[]{:S(2)}, u32[]{:S(2)}) collective-permute-start(bf16[32,4096]{1,0:T(8,128)(2,1)} %get-tuple-element.707), channel_id=1, source_target_pairs={{0,1},{1,2},{2,3},{3,4},{4,5},{5,6},{6,7},{8,9},{9,10},{10,11},{11... | collective-permute-start | bytes 786440 | tf_op jit(solution)/shard_map/while/body/eval_jaxpr/ppermute | solution.py:16
  158.2 1.3 collective-permute-done.1
  159.6 7.0 %conditional.9 = (bf16[2,32,4096]{2,1,0:T(8,128)(2,1)}, bf16[2,32,4096]{2,1,0:T(8,128)(2,1)}, bf16[2,32,128]{2,1,0:T(8,128)(2,1)}, bf16[1,32,4096]{2,1,0:T(8,128)(2,1)}) conditional(s32[]{:T(128)} %convert_element_type.165, (bf16[2,32,4096]{2,1,0:T(8,128)(2,1)}, bf16[2,32,4096]{2,1,0:T(8,128)(2,1)}, bf16[2,32,128]{2,1,0:T(8,128)(2,1)}) %tuple.108, ...), branch_computations={%region_7.7_spmd, %region_8.8_spmd} | conditional | flops 67903488 | bytes 6334044 | solution.py:131
  161.3 1.7 bitcast_dynamic-update-slice_fusion.4
  163.1 2.2 bitcast_dynamic-update-slice_fusion.5
  167.3 1.9 pad_maximum_fusion.4
  169.2 1.9 slice_bitcast_fusion.6
  172.3 12.2 %collective-permute-start = (bf16[32,4096]{1,0:T(8,128)(2,1)}, bf16[32,4096]{1,0:T(8,128)(2,1)}, u32[]{:S(2)}, u32[]{:S(2)}) collective-permute-start(bf16[32,4096]{1,0:T(8,128)(2,1)} %get-tuple-element.707), channel_id=1, source_target_pairs={{0,1},{1,2},{2,3},{3,4},{4,5},{5,6},{6,7},{8,9},{9,10},{10,11},{11... | collective-permute-start | bytes 786440 | tf_op jit(solution)/shard_map/while/body/eval_jaxpr/ppermute | solution.py:16
  184.6 3.3 collective-permute-done.1
  187.8 7.0 %conditional.9 = (bf16[2,32,4096]{2,1,0:T(8,128)(2,1)}, bf16[2,32,4096]{2,1,0:T(8,128)(2,1)}, bf16[2,32,128]{2,1,0:T(8,128)(2,1)}, bf16[1,32,4096]{2,1,0:T(8,128)(2,1)}) conditional(s32[]{:T(128)} %convert_element_type.165, (bf16[2,32,4096]{2,1,0:T(8,128)(2,1)}, bf16[2,32,4096]{2,1,0:T(8,128)(2,1)}, bf16[2,32,128]{2,1,0:T(8,128)(2,1)}) %tuple.108, ...), branch_computations={%region_7.7_spmd, %region_8.8_spmd} | conditional | flops 67903488 | bytes 6334044 | solution.py:131
  189.6 1.7 bitcast_dynamic-update-slice_fusion.4
  191.4 2.2 bitcast_dynamic-update-slice_fusion.5
  195.6 1.9 pad_maximum_fusion.4
  197.5 1.9 convolution_bitcast_fusion
  199.4 1.5 convolution_bitcast_fusion.1
  200.9 3.8 pad_maximum_fusion.1
  204.7 13.1 %copy.31 = f32[4096,2,2,128]{3,2,1,0:T(2,128)} copy(f32[4096,2,2,128]{0,3,1,2:T(8,128)} %pad_maximum_fusion.1) | data formatting | bytes 16777216 | tf_op jit(solution)/shard_map/stack | solution.py:165
  217.8 11.5 %reshape_reshape_reshape.3 = f32[4,16,2,32,512]{4,3,2,1,0:T(8,128)} reshape(f32[4096,2,2,128]{3,2,1,0:T(2,128)} %copy.31) | data formatting | bytes 16777216 | tf_op jit(solution)/shard_map/reshape;reshape;reshape | solution.py:21
  229.3 8.5 %copy.32 = f32[2,16,4,32,512]{4,3,2,1,0:T(8,128)} copy(f32[2,16,4,32,512]{4,3,0,1,2:T(8,128)} %bitcast.196) | data formatting | bytes 16777216 | tf_op jit(solution)/shard_map/transpose | solution.py:22
  237.8 53.0 %reduce-scatter.4.cloned.1.call-done = f32[64,32,512]{2,1,0:T(8,128)} async-done(((f32[128,32,512]{2,1,0:T(8,128)}), f32[64,32,512]{2,1,0:T(8,128)}) %reduce-scatter.4.cloned.1.call-update) | async-done | bytes 4194320 | tf_op jit(solution)/shard_map/reduce_scatter | solution.py:25
  290.9 77.0 %reduce-scatter.6.cloned.1.call-done = f32[4,32,512]{2,1,0:T(8,128)} async-done(((f32[64,32,512]{2,1,0:T(8,128)}), f32[4,32,512]{2,1,0:T(8,128)}) %reduce-scatter.6.cloned.1.call-update) | async-done | bytes 262160 | tf_op jit(solution)/shard_map/reduce_scatter | solution.py:25
  367.9 2.3 maximum_bitcast_fusion
  370.2 39.9 %reduce-scatter.8.cloned.1.call-done = f32[1,32,512]{2,1,0:T(8,128)} async-done(((f32[4,32,512]{2,1,0:T(8,128)}), f32[1,32,512]{2,1,0:T(8,128)}) %reduce-scatter.8.cloned.1.call-update) | async-done | bytes 65552 | tf_op jit(solution)/shard_map/reduce_scatter | solution.py:25
  411.0 3.3 all-gather
  414.3 9.4 %all-gather.1 = bf16[8,1,32,2,128]{4,2,3,1,0:T(8,128)(2,1)S(1)} all-gather(bf16[2,1,32,2,128]{4,2,3,1,0:T(8,128)(2,1)S(1)} %copy.33), channel_id=3, replica_groups=mesh['dp_0'=4,'dp_1'=16,'dp_2'=2,'section_0'=2,'section_1'=4] {'section_1'}, dimensions={0}, use_global_device_ids=true | all-gather | bytes 163840 | tf_op jit(solution)/shard_map/all_gather | solution.py:48
  (84 shorter events, 48.3 us)
Async XLA Ops:
  7.2 5.1 %copy-start = (bf16[1,2,2,32,4096]{4,3,2,1,0:T(8,128)(2,1)S(1)}, bf16[1,2,2,32,4096]{4,3,2,1,0:T(8,128)(2,1)}, u32[]{:S(2)}) copy-start(bf16[1,2,2,32,4096]{4,3,2,1,0:T(8,128)(2,1)} %param.16) | copy-start | bytes 3145732
  7.2 283.6 %reduce-scatter.4.cloned.1.call-start = ((), (), s32[]{:S(2)}) async-start(), calls=%async_computation.3 | async-start | bytes 12582912 | tf_op jit(solution)/shard_map/reduce_scatter | solution.py:25
  21.7 3.9 copy-start.3
  30.0 7.3 %collective-permute-start.1 = (bf16[32,4096]{1,0:T(8,128)(2,1)}, bf16[32,4096]{1,0:T(8,128)(2,1)S(1)}, u32[]{:S(2)}, u32[]{:S(2)}) collective-permute-start(bf16[32,4096]{1,0:T(8,128)(2,1)} %get-tuple-element.709), channel_id=1, source_target_pairs={{1,0},{2,1},{3,2},{4,3},{5,4},{6,5},{7,6},{9,8},{10,9},{11,10},{12... | collective-permute-start | bytes 786440 | tf_op jit(solution)/shard_map/while/body/eval_jaxpr/ppermute | solution.py:16
  31.3 7.6 %collective-permute-start = (bf16[32,4096]{1,0:T(8,128)(2,1)}, bf16[32,4096]{1,0:T(8,128)(2,1)}, u32[]{:S(2)}, u32[]{:S(2)}) collective-permute-start(bf16[32,4096]{1,0:T(8,128)(2,1)} %get-tuple-element.707), channel_id=1, source_target_pairs={{0,1},{1,2},{2,3},{3,4},{4,5},{5,6},{6,7},{8,9},{9,10},{10,11},{11... | collective-permute-start | bytes 786440 | tf_op jit(solution)/shard_map/while/body/eval_jaxpr/ppermute | solution.py:16
  48.0 8.7 %collective-permute-start.1 = (bf16[32,4096]{1,0:T(8,128)(2,1)}, bf16[32,4096]{1,0:T(8,128)(2,1)S(1)}, u32[]{:S(2)}, u32[]{:S(2)}) collective-permute-start(bf16[32,4096]{1,0:T(8,128)(2,1)} %get-tuple-element.709), channel_id=1, source_target_pairs={{1,0},{2,1},{3,2},{4,3},{5,4},{6,5},{7,6},{9,8},{10,9},{11,10},{12... | collective-permute-start | bytes 786440 | tf_op jit(solution)/shard_map/while/body/eval_jaxpr/ppermute | solution.py:16
  49.3 9.0 %collective-permute-start = (bf16[32,4096]{1,0:T(8,128)(2,1)}, bf16[32,4096]{1,0:T(8,128)(2,1)}, u32[]{:S(2)}, u32[]{:S(2)}) collective-permute-start(bf16[32,4096]{1,0:T(8,128)(2,1)} %get-tuple-element.707), channel_id=1, source_target_pairs={{0,1},{1,2},{2,3},{3,4},{4,5},{5,6},{6,7},{8,9},{9,10},{10,11},{11... | collective-permute-start | bytes 786440 | tf_op jit(solution)/shard_map/while/body/eval_jaxpr/ppermute | solution.py:16
  62.7 13.3 %collective-permute-start.1 = (bf16[32,4096]{1,0:T(8,128)(2,1)}, bf16[32,4096]{1,0:T(8,128)(2,1)S(1)}, u32[]{:S(2)}, u32[]{:S(2)}) collective-permute-start(bf16[32,4096]{1,0:T(8,128)(2,1)} %get-tuple-element.709), channel_id=1, source_target_pairs={{1,0},{2,1},{3,2},{4,3},{5,4},{6,5},{7,6},{9,8},{10,9},{11,10},{12... | collective-permute-start | bytes 786440 | tf_op jit(solution)/shard_map/while/body/eval_jaxpr/ppermute | solution.py:16
  64.0 13.6 %collective-permute-start = (bf16[32,4096]{1,0:T(8,128)(2,1)}, bf16[32,4096]{1,0:T(8,128)(2,1)}, u32[]{:S(2)}, u32[]{:S(2)}) collective-permute-start(bf16[32,4096]{1,0:T(8,128)(2,1)} %get-tuple-element.707), channel_id=1, source_target_pairs={{0,1},{1,2},{2,3},{3,4},{4,5},{5,6},{6,7},{8,9},{9,10},{10,11},{11... | collective-permute-start | bytes 786440 | tf_op jit(solution)/shard_map/while/body/eval_jaxpr/ppermute | solution.py:16
  82.1 7.8 %collective-permute-start.1 = (bf16[32,4096]{1,0:T(8,128)(2,1)}, bf16[32,4096]{1,0:T(8,128)(2,1)S(1)}, u32[]{:S(2)}, u32[]{:S(2)}) collective-permute-start(bf16[32,4096]{1,0:T(8,128)(2,1)} %get-tuple-element.709), channel_id=1, source_target_pairs={{1,0},{2,1},{3,2},{4,3},{5,4},{6,5},{7,6},{9,8},{10,9},{11,10},{12... | collective-permute-start | bytes 786440 | tf_op jit(solution)/shard_map/while/body/eval_jaxpr/ppermute | solution.py:16
  83.4 8.1 %collective-permute-start = (bf16[32,4096]{1,0:T(8,128)(2,1)}, bf16[32,4096]{1,0:T(8,128)(2,1)}, u32[]{:S(2)}, u32[]{:S(2)}) collective-permute-start(bf16[32,4096]{1,0:T(8,128)(2,1)} %get-tuple-element.707), channel_id=1, source_target_pairs={{0,1},{1,2},{2,3},{3,4},{4,5},{5,6},{6,7},{8,9},{9,10},{10,11},{11... | collective-permute-start | bytes 786440 | tf_op jit(solution)/shard_map/while/body/eval_jaxpr/ppermute | solution.py:16
  96.0 15.1 %collective-permute-start.1 = (bf16[32,4096]{1,0:T(8,128)(2,1)}, bf16[32,4096]{1,0:T(8,128)(2,1)S(1)}, u32[]{:S(2)}, u32[]{:S(2)}) collective-permute-start(bf16[32,4096]{1,0:T(8,128)(2,1)} %get-tuple-element.709), channel_id=1, source_target_pairs={{1,0},{2,1},{3,2},{4,3},{5,4},{6,5},{7,6},{9,8},{10,9},{11,10},{12... | collective-permute-start | bytes 786440 | tf_op jit(solution)/shard_map/while/body/eval_jaxpr/ppermute | solution.py:16
  97.2 15.7 %collective-permute-start = (bf16[32,4096]{1,0:T(8,128)(2,1)}, bf16[32,4096]{1,0:T(8,128)(2,1)}, u32[]{:S(2)}, u32[]{:S(2)}) collective-permute-start(bf16[32,4096]{1,0:T(8,128)(2,1)} %get-tuple-element.707), channel_id=1, source_target_pairs={{0,1},{1,2},{2,3},{3,4},{4,5},{5,6},{6,7},{8,9},{9,10},{10,11},{11... | collective-permute-start | bytes 786440 | tf_op jit(solution)/shard_map/while/body/eval_jaxpr/ppermute | solution.py:16
  117.4 8.0 %collective-permute-start.1 = (bf16[32,4096]{1,0:T(8,128)(2,1)}, bf16[32,4096]{1,0:T(8,128)(2,1)S(1)}, u32[]{:S(2)}, u32[]{:S(2)}) collective-permute-start(bf16[32,4096]{1,0:T(8,128)(2,1)} %get-tuple-element.709), channel_id=1, source_target_pairs={{1,0},{2,1},{3,2},{4,3},{5,4},{6,5},{7,6},{9,8},{10,9},{11,10},{12... | collective-permute-start | bytes 786440 | tf_op jit(solution)/shard_map/while/body/eval_jaxpr/ppermute | solution.py:16
  118.7 8.3 %collective-permute-start = (bf16[32,4096]{1,0:T(8,128)(2,1)}, bf16[32,4096]{1,0:T(8,128)(2,1)}, u32[]{:S(2)}, u32[]{:S(2)}) collective-permute-start(bf16[32,4096]{1,0:T(8,128)(2,1)} %get-tuple-element.707), channel_id=1, source_target_pairs={{0,1},{1,2},{2,3},{3,4},{4,5},{5,6},{6,7},{8,9},{9,10},{10,11},{11... | collective-permute-start | bytes 786440 | tf_op jit(solution)/shard_map/while/body/eval_jaxpr/ppermute | solution.py:16
  131.5 28.1 %collective-permute-start.1 = (bf16[32,4096]{1,0:T(8,128)(2,1)}, bf16[32,4096]{1,0:T(8,128)(2,1)S(1)}, u32[]{:S(2)}, u32[]{:S(2)}) collective-permute-start(bf16[32,4096]{1,0:T(8,128)(2,1)} %get-tuple-element.709), channel_id=1, source_target_pairs={{1,0},{2,1},{3,2},{4,3},{5,4},{6,5},{7,6},{9,8},{10,9},{11,10},{12... | collective-permute-start | bytes 786440 | tf_op jit(solution)/shard_map/while/body/eval_jaxpr/ppermute | solution.py:16
  132.8 33.8 %collective-permute-start = (bf16[32,4096]{1,0:T(8,128)(2,1)}, bf16[32,4096]{1,0:T(8,128)(2,1)}, u32[]{:S(2)}, u32[]{:S(2)}) collective-permute-start(bf16[32,4096]{1,0:T(8,128)(2,1)} %get-tuple-element.707), channel_id=1, source_target_pairs={{0,1},{1,2},{2,3},{3,4},{4,5},{5,6},{6,7},{8,9},{9,10},{10,11},{11... | collective-permute-start | bytes 786440 | tf_op jit(solution)/shard_map/while/body/eval_jaxpr/ppermute | solution.py:16
  159.6 0.7 copy-start.1
  171.1 16.8 %collective-permute-start.1 = (bf16[32,4096]{1,0:T(8,128)(2,1)}, bf16[32,4096]{1,0:T(8,128)(2,1)S(1)}, u32[]{:S(2)}, u32[]{:S(2)}) collective-permute-start(bf16[32,4096]{1,0:T(8,128)(2,1)} %get-tuple-element.709), channel_id=1, source_target_pairs={{1,0},{2,1},{3,2},{4,3},{5,4},{6,5},{7,6},{9,8},{10,9},{11,10},{12... | collective-permute-start | bytes 786440 | tf_op jit(solution)/shard_map/while/body/eval_jaxpr/ppermute | solution.py:16
  172.3 22.5 %collective-permute-start = (bf16[32,4096]{1,0:T(8,128)(2,1)}, bf16[32,4096]{1,0:T(8,128)(2,1)}, u32[]{:S(2)}, u32[]{:S(2)}) collective-permute-start(bf16[32,4096]{1,0:T(8,128)(2,1)} %get-tuple-element.707), channel_id=1, source_target_pairs={{0,1},{1,2},{2,3},{3,4},{4,5},{5,6},{6,7},{8,9},{9,10},{10,11},{11... | collective-permute-start | bytes 786440 | tf_op jit(solution)/shard_map/while/body/eval_jaxpr/ppermute | solution.py:16
  187.8 0.7 copy-start.1
  237.8 130.1 %reduce-scatter.6.cloned.1.call-start = ((), (), s32[]{:S(2)}) async-start(), calls=%async_computation.4 | async-start | bytes 4456448 | tf_op jit(solution)/shard_map/reduce_scatter | solution.py:25
  290.8 119.3 %reduce-scatter.8.cloned.1.call-start = ((), (), s32[]{:S(2)}) async-start(), calls=%async_computation.5 | async-start | bytes 327680 | tf_op jit(solution)/shard_map/reduce_scatter | solution.py:25
Sparse Core Ops, SparseCore 0:
  237.9 52.8 reduce-scatter.3
  294.2 73.6 reduce-scatter.5
  371.3 38.7 reduce-scatter.7
where the time goes:
time: 438 us; the launch traced here: 431 us
  waiting for transfers between devices  190 us (43%)
  starting transfers between devices  91.1 us (21%)
  local copies, waits for them, and re-layouts  74.3 us (17%)
  other arithmetic  27.9 us (6%)
  matrix products  21.6 us (5%)
  between operations  13.8 us (3%)
  blocking collectives  12.7 us (3%)
    reduce_scatter x3, waiting for transfers between devices, sum_in_order(): blocks = lax.psum_scatter(blocks, axes[k], scatter_dimension=0, tiled=True)  170 us
    ppermute x16, starting transfers between devices, passed_along(): return lax.ppermute(block, axis, route)  91 us
    ppermute x16, waiting for transfers between devices, passed_along(): return lax.ppermute(block, axis, route)  19.5 us
    another operation x9, other arithmetic, advance(): return (jnp.stack(outgoing), tuple(updated))  16.8 us
    squeeze x8, local copies, waits for them, and re-layouts, loop_body(): from_next = passed_along(outgoing[0], SECTION, -1)  15 us
    another operation x1, local copies, waits for them, and re-layouts, shards(): jnp.stack([grad_value, grad_output], axis=2)  13.1 us
    all_gather x2, blocking collectives, stacked_from(): blocks = lax.all_gather(blocks, axes[k])  12.7 us
    another operation x1, local copies, waits for them, and re-layouts, sum_in_order(): blocks = blocks.reshape(*lengths, *blocks.shape[1:])  11.5 us
  transfers between devices with their start and end apart: 19, of which 17 were waited for; matrix products, arithmetic and copies ran while one was open for 4% of the time, Pallas kernels for 0%

commit v1 on v0

v1 whole, which is shorter than its diff:
```python
import math

import jax
import jax.numpy as jnp
from jax import lax
from jax.experimental import pallas as pl
from jax.experimental.pallas import tpu as pltpu
from jax.sharding import Mesh
from jax.sharding import PartitionSpec as P

SECTION = ("section_0", "section_1")
DP = ("dp_0", "dp_1", "dp_2")
MESH = pl.DeviceIdType.MESH
F32 = jnp.float32
BF16 = jnp.bfloat16
UNIT = 16


def transposed_attention(q, k, length_0, length_1):
    total = q.shape[0]
    half = total // 2
    scores = lax.dot_general(k, q, (((1,), (1,)), ((), ())), preferred_element_type=F32)
    scores = scores / math.sqrt(q.shape[1])
    key_pos = lax.broadcasted_iota(jnp.int32, (total, total), 0)
    query_pos = lax.broadcasted_iota(jnp.int32, (total, total), 1)
    limit = jnp.where(key_pos < half, length_0, length_1 + half)
    first = jnp.where(query_pos < half, 0, half)
    allowed = (key_pos <= query_pos) & (key_pos >= first) & (key_pos < limit)
    scores = jnp.where(allowed, scores, -1e30)
    top = jnp.max(scores, axis=0, keepdims=True)
    raised = jnp.where(allowed, jnp.exp(scores - top), 0.0)
    return (raised / jnp.sum(raised, axis=0, keepdims=True)).astype(BF16)


def make_kernel(n_y, n_z, n_x, sections, width, tokens, head):
    units = tokens // UNIT
    half_z = n_z // 2
    rows = width // (n_y * n_z)
    slab = width // n_y
    half_rows = rows // 2
    tile = min(1024, width)

    def kernel(
        lengths, q_ref, k_ref, x_hbm, w_hbm, cot_hbm, g_hbm, out_ref,
        wv, wo, acts, small, att, og, grads, part, ring_out, ring_in, y_out, y_in, z_sum,
        f_out, f_in, w_sem, x_sem, chain_send, chain_recv, g_sem, pair_send, pair_recv,
        rhs_send, rhs_recv, ring_send, ring_recv, y_send, y_recv, f_send, f_recv,
    ):
        y = lax.axis_index("dp_0")
        z = lax.axis_index("dp_1")
        core = lax.axis_index("dp_2")
        position = lax.axis_index("section_0") * n_x + lax.axis_index("section_1")
        other = 1 - core

        def at_position(j):
            return {"section_0": j // n_x, "section_1": j % n_x}

        partner = {"dp_2": other}
        z_next = {"dp_1": (z + 1) % n_z}
        z_prev = {"dp_1": (z + n_z - 1) % n_z}
        mirror = at_position(sections - 1 - position)
        mirror_other = {**mirror, "dp_2": other}
        y_peers = [{"dp_0": (y + d) % n_y} for d in range(1, n_y)]
        ahead = at_position((position + 1) % sections)
        behind = at_position((position + sections - 1) % sections)

        barrier = pltpu.get_barrier_semaphore()
        friends = [partner, z_next, z_prev, mirror, mirror_other, ahead, behind] + y_peers
        for friend in friends:
            pl.semaphore_signal(barrier, inc=1, device_id=friend, device_id_type=MESH)

        def row_of(m):
            half = units // 2
            return pl.multiple_of((1 - m // half) * UNIT + (m % half) * 2 * UNIT, UNIT)

        def cot_copy(r, m):
            at = pl.ds(row_of(m), UNIT)
            return pltpu.make_async_copy(
                cot_hbm.at[r, at], acts.at[0, r, at], chain_recv.at[r, m]
            )

        w_copies = []
        for r in range(2):
            w_copies.append(pltpu.make_async_copy(w_hbm.at[r, 1], wo.at[r], w_sem.at[r, 1]))
            w_copies.append(pltpu.make_async_copy(w_hbm.at[r, 0], wv.at[r], w_sem.at[r, 0]))
        x_copy = pltpu.make_async_copy(x_hbm, acts.at[1], x_sem)

        @pl.when(position == sections - 1)
        def _():
            for m in range(units):
                cot_copy(0, m).start()

        @pl.when(position == 0)
        def _():
            for m in range(units):
                cot_copy(1, m).start()

        for copy in w_copies:
            copy.start()
        x_copy.start()

        for r in range(2):
            att[r] = transposed_attention(q_ref[r], k_ref[r], lengths[r, 0], lengths[r, 1])
        og[...] = jnp.zeros_like(og)
        for copy in w_copies:
            copy.wait()
        x_copy.wait()
        pl.semaphore_wait(barrier, len(friends))

        def mixtures():
            for r in range(2):
                values = jnp.dot(acts[1, r], wv[r], preferred_element_type=F32).astype(BF16)
                small[0, r] = lax.dot_general(
                    att[r], values, (((0,), (0,)), ((), ())), preferred_element_type=F32
                ).astype(BF16)

        mid = (position != 0) & (position != sections - 1)

        @pl.when(mid)
        def _():
            mixtures()

        first = jnp.where(position < sections // 2, 1, 0)

        def goes_on(r):
            return jnp.where(r == 0, position > 0, position < sections - 1)

        def chain_copy(r, m):
            at = pl.ds(row_of(m), UNIT)
            return pltpu.make_async_remote_copy(
                src_ref=grads.at[r, at],
                dst_ref=acts.at[0, r, at],
                send_sem=chain_send.at[r, m],
                recv_sem=chain_recv.at[r, m],
                device_id=at_position(
                    jnp.clip(position + jnp.where(r == 0, -1, 1), 0, sections - 1)
                ),
                device_id_type=MESH,
            )

        def out_copy(r, m):
            at = pl.ds(row_of(m), UNIT)
            return pltpu.make_async_copy(grads.at[r, at], g_hbm.at[r, at], g_sem.at[r, m])

        def pair_copy(r, m):
            at = pl.ds(row_of(m), UNIT)
            return pltpu.make_async_remote_copy(
                src_ref=acts.at[core, r, at],
                dst_ref=acts.at[2, r, at],
                send_sem=pair_send.at[r, m],
                recv_sem=pair_recv.at[r, m],
                device_id=partner,
                device_id_type=MESH,
            )

        def rhs_copy(r):
            return pltpu.make_async_remote_copy(
                src_ref=small.at[core, r],
                dst_ref=small.at[2, r],
                send_sem=rhs_send.at[r],
                recv_sem=rhs_recv.at[r],
                device_id=partner,
                device_id_type=MESH,
            )

        def unit(r, m):
            at = pl.ds(row_of(m), UNIT)
            cot_copy(r, m).wait()
            pair_copy(r, m).start()
            og[r, at] = jnp.dot(acts[0, r, at], wo[r], preferred_element_type=F32).astype(BF16)
            val_grad = jnp.dot(att[r, at], og[r], preferred_element_type=F32).astype(BF16)
            small[1, r, at] = val_grad
            for t in range(width // tile):
                cols = pl.ds(t * tile, tile)
                branch = lax.dot_general(
                    val_grad, wv[r, cols], (((1,), (1,)), ((), ())), preferred_element_type=F32
                )
                grads[r, at, cols] = (acts[0, r, at, cols].astype(F32) + branch).astype(BF16)

            @pl.when(goes_on(r))
            def _():
                chain_copy(r, m).start()

            out_copy(r, m).start()

        @pl.loop(0, units)
        def _(m):
            unit(first, m)

        @pl.when(jnp.logical_not(mid))
        def _():
            mixtures()

        rhs_copy(first).start()

        @pl.loop(0, units)
        def _(m):
            unit(1 - first, m)

        rhs_copy(1 - first).start()

        def products(r):
            rhs_copy(r).wait_recv()

            @pl.loop(0, units)
            def _(m):
                pair_copy(r, m).wait_recv()

            for t in range(n_y):
                cols = pl.ds(t * slab, slab)
                product = lax.dot_general(
                    acts[other, r, :, cols], small[other, r],
                    (((0,), (0,)), ((), ())), preferred_element_type=F32,
                ) + lax.dot_general(
                    acts[2, r, :, cols], small[2, r],
                    (((0,), (0,)), ((), ())), preferred_element_type=F32,
                )
                part[r, t] = product.reshape(n_z, rows, head)

        products(first)
        products(1 - first)

        def ring_copy(way, r, s):
            return pltpu.make_async_remote_copy(
                src_ref=ring_out.at[way, r, s],
                dst_ref=ring_in.at[way, r, s],
                send_sem=ring_send.at[way, r, s],
                recv_sem=ring_recv.at[way, r, s],
                device_id=z_next if way == 0 else z_prev,
                device_id_type=MESH,
            )

        def ring_step(way, r, s, starts):
            shift = half_z - s if way == 0 else half_z + s
            target = lax.rem(z + shift, n_z)
            total = part[r, :, pl.ds(target, 1)].reshape(n_y, rows, head)
            if not starts:
                ring_copy(way, r, s - 1).wait_recv()
                total = total + ring_in[way, r, s - 1].astype(F32)
            ring_out[way, r, s] = total.astype(BF16)
            ring_copy(way, r, s).start()

        ring_step(0, 0, 0, True)
        ring_step(1, 1, 0, True)
        ring_step(1, 0, 1, True)
        ring_step(0, 1, 1, True)
        ring_step(0, 0, 1, False)
        ring_step(1, 1, 1, False)

        @pl.loop(2, half_z)
        def _(s):
            for way, r in ((1, 0), (0, 1), (0, 0), (1, 1)):
                ring_step(way, r, s, False)

        for r in range(2):
            total = part[r, :, pl.ds(z, 1)].reshape(n_y, rows, head)
            for way in range(2):
                ring_copy(way, r, half_z - 1).wait_recv()
                total = total + ring_in[way, r, half_z - 1].astype(F32)
            z_sum[:, r] = total

        def y_copy(d):
            return pltpu.make_async_remote_copy(
                src_ref=y_out.at[d - 1],
                dst_ref=y_in.at[d - 1],
                send_sem=y_send.at[d - 1],
                recv_sem=y_recv.at[d - 1],
                device_id=y_peers[d - 1],
                device_id_type=MESH,
            )

        for d in range(1, n_y):
            y_out[d - 1] = z_sum[lax.rem(y + d, n_y)].astype(BF16)
            y_copy(d).start()
        total = z_sum[y]
        for d in range(1, n_y):
            y_copy(d).wait_recv()
            total = total + y_in[d - 1].astype(F32)
        z_sum[y] = total

        def f_copy(slot):
            return pltpu.make_async_remote_copy(
                src_ref=f_out.at[slot],
                dst_ref=f_in.at[slot],
                send_sem=f_send.at[slot],
                recv_sem=f_recv.at[slot],
                device_id=(partner, mirror, mirror_other)[slot],
                device_id_type=MESH,
            )

        mine = pl.ds(pl.multiple_of(core * half_rows, half_rows), half_rows)
        theirs = pl.ds(pl.multiple_of(other * half_rows, half_rows), half_rows)
        f_out[1] = z_sum[y, 1, mine]
        f_copy(1).start()
        f_out[2] = z_sum[y, 1, theirs]
        f_copy(2).start()
        f_out[0] = z_sum[y, 0, theirs]
        f_copy(0).start()
        for slot in range(3):
            f_copy(slot).wait_recv()
        out_ref[core] = z_sum[y, 0, mine] + f_in[1]
        out_ref[other] = f_in[0] + f_in[2]

        for slot in range(3):
            f_copy(slot).wait_send()
        for d in range(1, n_y):
            y_copy(d).wait_send()
        for way, r in ((0, 0), (1, 1), (1, 0), (0, 1)):
            begin = 0 if way == r else 1

            @pl.loop(begin, half_z)
            def _(s):
                ring_copy(way, r, s).wait_send()

        for r in range(2):
            rhs_copy(r).wait_send()

            @pl.loop(0, units)
            def _(m):
                pair_copy(r, m).wait_send()
                out_copy(r, m).wait()

                @pl.when(goes_on(r))
                def _():
                    chain_copy(r, m).wait_send()

    dma = pltpu.SemaphoreType.DMA
    vmem = pltpu.VMEM
    scratch = [
        vmem((2, width, head), BF16),
        vmem((2, width, head), BF16),
        vmem((3, 2, tokens, width), BF16),
        vmem((3, 2, tokens, head), BF16),
        vmem((2, tokens, tokens), BF16),
        vmem((2, tokens, head), BF16),
        vmem((2, tokens, width), BF16),
        vmem((2, n_y, n_z, rows, head), F32),
        vmem((2, 2, half_z, n_y, rows, head), BF16),
        vmem((2, 2, half_z, n_y, rows, head), BF16),
        vmem((n_y - 1, 2, rows, head), BF16),
        vmem((n_y - 1, 2, rows, head), BF16),
        vmem((n_y, 2, rows, head), F32),
        vmem((3, half_rows, head), F32),
        vmem((3, half_rows, head), F32),
        dma((2, 2)),
        dma,
        dma((2, units)),
        dma((2, units)),
        dma((2, units)),
        dma((2, units)),
        dma((2, units)),
        dma((2,)),
        dma((2,)),
        dma((2, 2, half_z)),
        dma((2, 2, half_z)),
        dma((n_y - 1,)),
        dma((n_y - 1,)),
        dma((3,)),
        dma((3,)),
    ]
    any_space = pl.BlockSpec(memory_space=pl.ANY)
    in_vmem = pl.BlockSpec(memory_space=pltpu.VMEM)
    return pl.pallas_call(
        kernel,
        out_shape=(
            jax.ShapeDtypeStruct((2, tokens, width), BF16),
            jax.ShapeDtypeStruct((2, half_rows, head), F32),
        ),
        in_specs=[
            pl.BlockSpec(memory_space=pltpu.SMEM),
            in_vmem,
            in_vmem,
            any_space,
            any_space,
            any_space,
        ],
        out_specs=(any_space, in_vmem),
        scratch_shapes=scratch,
        compiler_params=pltpu.CompilerParams(
            collective_id=0, has_side_effects=True, vmem_limit_bytes=56 * 2**20
        ),
    )


def shards(layer_inputs, saved_queries, saved_keys, held_weights, cotangent, valid_lengths):
    _, _, seqs, length, width = layer_inputs.shape
    head = saved_queries.shape[-1]
    tokens = seqs * length
    call = make_kernel(
        lax.axis_size("dp_0"),
        lax.axis_size("dp_1"),
        lax.axis_size("section_1"),
        lax.axis_size(SECTION),
        width,
        tokens,
        head,
    )
    grads, weight_grads = call(
        valid_lengths,
        saved_queries.reshape(2, tokens, head),
        saved_keys.reshape(2, tokens, head),
        layer_inputs.reshape(2, tokens, width),
        held_weights[0],
        cotangent.reshape(2, tokens, width),
    )
    return (grads.reshape(1, 2, seqs, length, width), weight_grads[None])


def on_mesh(finer):
    in_specs = (
        P(SECTION, None, DP, None, None),
        P(SECTION, None, DP, None, None),
        P(SECTION, None, DP, None, None),
        P(SECTION, None, None, None, None),
        P(None, DP, None, None),
        P(None, DP),
    )
    out_specs = (P(SECTION, None, DP, None, None), P(SECTION, None, DP, None))
    return jax.shard_map(
        shards, mesh=finer, in_specs=in_specs, out_specs=out_specs, check_vma=False
    )


def solution(mesh):
    return on_mesh(
        Mesh(
            mesh.devices.reshape(4, 16, 2, 2, 4),
            ("dp_0", "dp_1", "dp_2", "section_0", "section_1"),
        )
    )
```

time: 438 us -> 121 us (0.28); the launches traced: 431 us -> 121 us
  waiting for transfers between devices: 190 us -> 0 us
  Pallas kernels: 0 us -> 116 us
  starting transfers between devices: 91.1 us -> 0 us
  local copies, waits for them, and re-layouts: 74.3 us -> 3.66 us
  other arithmetic: 27.9 us -> 0 us
  matrix products: 21.6 us -> 0 us
  between operations: 13.8 us -> 0.64 us
  blocking collectives: 12.7 us -> 0 us
    reduce_scatter x3 -> x0, waiting for transfers between devices: 170 us -> none  [sum_in_order(): blocks = lax.psum_scatter(blocks, axes[k], scatter_dimension=0, tiled=True)]
    pallas_call x0 -> x1, Pallas kernels: none -> 116 us  [shards(): call(valid_lengths, saved_queries.reshape(2, tokens, head), saved_keys.re...]
    ppermute x16 -> x0, starting transfers between devices: 91 us -> none  [passed_along(): return lax.ppermute(block, axis, route)]
    another operation x18 -> x0, local copies, waits for them, and re-layouts: 34.9 us -> none  [the longest x1 13.1 us: shards(): jnp.stack([grad_value, grad_output], axis=2)]
    dot_general x11 -> x0, matrix products: 20.6 us -> none  [the longest x4 8.99 us: compute(): jnp.einsum('ts,th->sh', weights_now, out_grad, preferred_element_type=jnp...]
    another operation x10 -> x0, other arithmetic: 20.6 us -> none  [the longest x9 16.8 us: advance(): return (jnp.stack(outgoing), tuple(updated))]
    ppermute x16 -> x0, waiting for transfers between devices: 19.5 us -> none  [passed_along(): return lax.ppermute(block, axis, route)]
    squeeze x9 -> x0, local copies, waits for them, and re-layouts: 18.8 us -> none  [the longest x8 15 us: loop_body(): from_next = passed_along(outgoing[0], SECTION, -1)]
  transfers between devices with their start and end apart: 19 -> 0, of which waited for: 17 -> 0; matrix products, arithmetic and copies ran while one was open for 4% -> 0% of each run, Pallas kernels for 0% -> 0%
where the time goes in v1:
time: 121 us
  Pallas kernels  116 us (96%)
  local copies, waits for them, and re-layouts  3.66 us (3%)
    pallas_call x1, Pallas kernels, shards(): call(valid_lengths, saved_queries.reshape(2, tokens, head), saved_keys.re...  116 us
    unnamed x2, local copies, waits for them, and re-layouts  3.66 us

profile of v1, /device:TPU:1, one launch (start us, length us, event | category | flops | bytes accessed | tf_op | source)
XLA Modules:
  0.0 120.7 jit_solution(9164296731563279840)
XLA Ops:
  0.6 116.4 %shard_map.77 = (bf16[2,64,4096]{2,1,0:T(8,128)(2,1)}, f32[2,32,128]{2,1,0:T(8,128)}) custom-call(s32[2,2]{1,0:T(2,128)} %lengths.1, bf16[2,64,128]{2,1,0:T(8,128)(2,1)} %bitcast.11, bf16[2,64,128]{2,1,0:T(8,128)(2,1)} %bitcast.12, bf16[2,64,4096]{2,1,0:T(8,128)(2,1)} %bitcast.9, bf16[2,2,4096,128]{3,2,1,0:T(8,128)(2,1)} %bitcast.7, ...), custom_call_target="tpu_custom_call" | custom-call | tf_op jit(solution)/shard_map/pallas_call | solution.py:398
  117.0 2.3 %copy.10 = bf16[1,2,2,32,4096]{4,3,2,1,0:T(8,128)(2,1)} copy(bf16[1,2,2,32,4096]{4,3,2,1,0:T(8,128)(2,1)} %bitcast.8) | data formatting | bytes 2097152
  119.3 1.4 %copy.11 = f32[1,2,32,128]{3,2,1,0:T(8,128)} copy(f32[1,2,32,128]{3,2,1,0:T(8,128)} %bitcast.13) | data formatting | bytes 65536
